TPU v7x, 128 devices: a whole 4x4x4 slice. The times are simulated.
128 devices in a mesh: req: 8 (over x, core), mlp: 16 (over z, y).
Axes of the slice: x: 4, y: 4, z: 4, core: 2. Of those that a mesh axis runs over, the one named last changes fastest.
Arguments:
- tokens: bfloat16 [8192, 4096], P(('req', 'mlp')), may hold values from -6 to 6
- layer_norm_gain: float32 [4096], replicated, may hold values from 0.1 to 1.9
- layer_norm_bias: float32 [4096], replicated, may hold values from -2 to 2
- query_key_weight: bfloat16 [4096, 16, 768], P(None, 'mlp')
- output_weight: bfloat16 [16, 256, 4096], P('mlp'), may hold values from -0.09375 to 0.09375
- up_weight: bfloat16 [4096, 8192], P(None, 'mlp'), may hold values from -0.09375 to 0.09375
- input_bias: float32 [8192], P('mlp'), may hold values from -3 to 3
- down_weight: bfloat16 [8192, 4096], P('mlp'), may hold values from -0.0625 to 0.0625
- output_bias: float32 [4096], replicated, may hold values from -2 to 2
- input_adapter_left: bfloat16 [4096, 2048], P(None, 'mlp'), may hold values from -0.09375 to 0.09375
- query_key_value_right: bfloat16 [1024, 16, 768], P(None, 'mlp'), may hold values from -1.5 to 1.5
- up_adapter_right: bfloat16 [1024, 8192], P(None, 'mlp'), may hold values from -1.5 to 1.5
- output_adapter_left: bfloat16 [16, 256, 1024], P('mlp'), may hold values from -0.09375 to 0.09375
- down_adapter_left: bfloat16 [8192, 1024], P('mlp'), may hold values from -0.0625 to 0.0625
- output_adapter_right: bfloat16 [2048, 4096], P('mlp'), may hold values from -1 to 1
- lengths: int32 [257], replicated, may hold values from 8 to 4096, as said below
- request_adapter: int32 [257], replicated, may hold values from 0 to 63
- slot_adapter: int32 [64], P('mlp'), may hold values from 0 to 63, each once
Outputs:
- mixed: bfloat16 [8192, 4096], P(('req', 'mlp'))
Inputs may be any that keep to these rules, and one draw needn't show every extreme that they name: `lengths`: one request holds exactly 4096 tokens, every other one 8 to 24; together they hold 8192 tokens. `slot_adapter`: every adapter id stands in exactly one slot.
All inputs are finite; a program needn't handle non-finite values.
Results may differ from a plain program's by a relative error of at most 0.017.
Values may be sent and summed in bfloat16 or wider, within the bound.
A program may use at most 128 MiB of HBM per device.

v0:
```python
import math
import jax
import jax.numpy as jnp
from jax import lax
from jax.sharding import PartitionSpec as P

HEAD_SIZE = 256
ROT = 64
ADAPTER_RANK = 16
ADP_DEV = 4
EPSILON = 1e-05
NEGATIVE_FILL = -1e30


def rank_product(left_side, right_side):
    return jnp.dot(left_side, right_side, preferred_element_type=jnp.float32)


def normalize(inputs, layer_norm_gain, layer_norm_bias):
    values = inputs.astype(jnp.float32)
    center = values - jnp.mean(values, axis=1, keepdims=True)
    spread = jnp.mean(center * center, axis=1, keepdims=True)
    scaled = center * lax.rsqrt(spread + EPSILON)
    return (scaled * layer_norm_gain + layer_norm_bias).astype(jnp.bfloat16)


def token_info(lengths, request_adapter, first_row, row_count):
    endings = jnp.cumsum(lengths)
    anchors = endings - lengths
    token_index = first_row + lax.iota(jnp.int32, row_count)
    inside = anchors[None, :] <= token_index[:, None]
    request = jnp.sum(inside.astype(jnp.int32), axis=1) - 1
    request_start = jnp.max(jnp.where(inside, anchors[None, :], jnp.zeros((), jnp.int32)), axis=1)
    adapter_id = jnp.take(request_adapter, jnp.maximum(request, 0))
    return (token_index, request, token_index - request_start, adapter_id)


def rotate(matrix, position):
    row_count = matrix.shape[0]
    head_count = matrix.shape[1]
    half_rot = ROT // 2
    frequency = jnp.exp(jnp.arange(half_rot, dtype=jnp.float32) * (-2.0 * math.log(10000.0) / ROT))
    angles = position.astype(jnp.float32)[:, None] * frequency[None, :]
    cosine = jnp.cos(angles)[:, None, :]
    sine_value = jnp.sin(angles)[:, None, :]
    paired_part = matrix[:, :, :ROT].reshape(row_count, head_count, half_rot, 2)
    even_part = paired_part[:, :, :, 0]
    odd_part = paired_part[:, :, :, 1]
    turned = jnp.stack(
        [even_part * cosine - odd_part * sine_value, odd_part * cosine + even_part * sine_value],
        axis=-1,
    )
    return jnp.concatenate([turned.reshape(row_count, head_count, ROT), matrix[:, :, ROT:]], axis=2)


def slot_selector(products, chosen, adapter_id, column_count):
    row_count = products.shape[0]
    selector = (adapter_id[:, None] == chosen[None, :]).astype(jnp.float32)
    reshaped = products.reshape(row_count, chosen.shape[0], column_count)
    return jnp.sum(selector[:, :, None] * reshaped, axis=1)


def widen_rows(values, chosen, adapter_id):
    selector = adapter_id[:, None] == chosen[None, :]
    spread = jnp.where(selector[:, :, None], values[:, None, :], jnp.zeros((), values.dtype))
    return spread.reshape(values.shape[0], chosen.shape[0] * values.shape[1])


def per_device(
    tokens,
    layer_norm_gain,
    layer_norm_bias,
    query_key_weight,
    output_weight,
    up_weight,
    input_bias,
    down_weight,
    output_bias,
    input_adapter_left,
    query_key_value_right,
    up_adapter_right,
    output_adapter_left,
    down_adapter_left,
    output_adapter_right,
    lengths,
    request_adapter,
    slot_adapter,
):
    tok_dev = tokens.shape[0]
    model_width = tokens.shape[1]
    mlp_count = lax.axis_size("mlp")
    tok_grp = tok_dev * mlp_count
    group_first = lax.axis_index("req") * tok_grp
    heads_local = query_key_weight.shape[1]
    hid_local = up_weight.shape[1]
    adapter_ids = slot_adapter.shape[0] * mlp_count
    every_id = lax.iota(jnp.int32, adapter_ids)
    query_key_columns = heads_local * 3 * HEAD_SIZE
    attention_columns = heads_local * HEAD_SIZE
    query_key_rows = query_key_weight.reshape(model_width, query_key_columns)
    normed_rows = normalize(tokens, layer_norm_gain, layer_norm_bias)
    slot_portion = lax.all_gather(normed_rows, "mlp", axis=0, tiled=True)
    grouped = jnp.concatenate(
        [
            rank_product(slot_portion, query_key_rows),
            rank_product(slot_portion, up_weight),
            rank_product(slot_portion, input_adapter_left),
        ],
        axis=1,
    )
    token_index, request, position, adapter_id = token_info(
        lengths, request_adapter, group_first, tok_grp
    )
    rank_part = slot_selector(
        grouped[:, query_key_columns + hid_local :], slot_adapter, adapter_id, 2 * ADAPTER_RANK
    )
    rank_input = lax.psum(rank_part.astype(jnp.bfloat16), "mlp")
    qkv_extra = rank_product(
        widen_rows(rank_input[:, :ADAPTER_RANK], every_id, adapter_id),
        query_key_value_right.reshape(adapter_ids * ADAPTER_RANK, query_key_columns),
    )
    up_delta = rank_product(
        widen_rows(rank_input[:, ADAPTER_RANK:], every_id, adapter_id), up_adapter_right
    )
    projected_rows = (grouped[:, :query_key_columns] + qkv_extra).reshape(
        tok_grp, heads_local, 3 * HEAD_SIZE
    )
    hidden_units = jax.nn.gelu(
        grouped[:, query_key_columns : query_key_columns + hid_local] + up_delta + input_bias,
        approximate=True,
    ).astype(jnp.bfloat16)
    queries = rotate(projected_rows[:, :, :HEAD_SIZE], position).astype(jnp.bfloat16)
    key_rows = (
        rotate(projected_rows[:, :, HEAD_SIZE : 2 * HEAD_SIZE], position)
        .astype(jnp.bfloat16)
        .reshape(tok_grp, attention_columns)
    )
    value_rows = (
        projected_rows[:, :, 2 * HEAD_SIZE :]
        .astype(jnp.bfloat16)
        .reshape(tok_grp, attention_columns)
    )
    paired = jnp.stack([key_rows, value_rows])
    score_scale = HEAD_SIZE ** (-0.5)
    last_row = group_first + tok_grp - 1
    start_state = (
        jnp.full((tok_grp, heads_local), NEGATIVE_FILL, jnp.float32),
        jnp.zeros((tok_grp, heads_local), jnp.float32),
        jnp.zeros((tok_grp, heads_local, HEAD_SIZE), jnp.float32),
    )
    slot_portion = lax.all_gather(paired, "req", axis=1, tiled=True)
    offset = jnp.int32(0)
    amount = slot_portion.shape[1]
    key_index, key_request, key_position, key_adapter = token_info(
        lengths, request_adapter, offset, amount
    )
    useful = jnp.logical_and(offset <= last_row, key_request[amount - 1] >= request[0])

    def attend(current):
        running_top, running_total, running_sum = current
        part_keys = slot_portion[0].reshape(amount, heads_local, HEAD_SIZE)
        part_values = slot_portion[1].reshape(amount, heads_local, HEAD_SIZE)
        scores = (
            jnp.einsum("qhd,khd->qhk", queries, part_keys, preferred_element_type=jnp.float32)
            * score_scale
        )
        allowed = jnp.logical_and(
            key_request[None, :] == request[:, None], key_index[None, :] <= token_index[:, None]
        )[:, None, :]
        masked = jnp.where(allowed, scores, NEGATIVE_FILL)
        new_top = jnp.maximum(running_top, jnp.max(masked, axis=2))
        weights = jnp.where(allowed, jnp.exp(masked - new_top[:, :, None]), 0.0)
        new_total = jnp.sum(weights, axis=2)
        new_sum = jnp.einsum(
            "qhk,khd->qhd",
            weights.astype(jnp.bfloat16),
            part_values,
            preferred_element_type=jnp.float32,
        )
        return (new_top, new_total, new_sum)

    final_state = lax.cond(useful, attend, lambda current: current, start_state)
    attention_output = (
        (final_state[2] / final_state[1][:, :, None])
        .astype(jnp.bfloat16)
        .reshape(tok_grp, attention_columns)
    )
    output_rows = output_weight.reshape(attention_columns, model_width)
    own_ids = lax.axis_index("mlp") * ADP_DEV + lax.iota(jnp.int32, ADP_DEV)
    output_rank_rows = rank_product(
        attention_output, output_adapter_left.reshape(attention_columns, adapter_ids * ADAPTER_RANK)
    )
    down_rank_rows = rank_product(hidden_units, down_adapter_left)
    rank_part_out = jnp.concatenate(
        [
            slot_selector(output_rank_rows, every_id, adapter_id, ADAPTER_RANK),
            slot_selector(down_rank_rows, every_id, adapter_id, ADAPTER_RANK),
        ],
        axis=1,
    )
    rank_output = lax.psum(rank_part_out.astype(jnp.bfloat16), "mlp")
    rank_widened = widen_rows(rank_output, own_ids, adapter_id)
    mixed = lax.psum_scatter(
        (
            rank_product(attention_output, output_rows)
            + (
                rank_product(hidden_units, down_weight)
                + rank_product(rank_widened, output_adapter_right)
            )
        ).astype(jnp.bfloat16),
        "mlp",
        scatter_dimension=0,
        tiled=True,
    ).astype(jnp.float32)
    return (mixed + tokens.astype(jnp.float32) + output_bias).astype(jnp.bfloat16)


def solution(mesh):
    in_specs = (
        P(("req", "mlp"), None),
        P(),
        P(),
        P(None, "mlp", None),
        P("mlp", None, None),
        P(None, "mlp"),
        P("mlp"),
        P("mlp", None),
        P(),
        P(None, "mlp"),
        P(None, "mlp", None),
        P(None, "mlp"),
        P("mlp", None, None),
        P("mlp", None),
        P("mlp", None),
        P(),
        P(),
        P("mlp"),
    )
    out_specs = P(("req", "mlp"), None)
    return jax.shard_map(
        per_device, mesh=mesh, in_specs=in_specs, out_specs=out_specs, check_vma=False
    )
```

profile of v0, /device:TPU:0, one launch (start us, length us, event | category | flops | bytes accessed | tf_op | source)
XLA Modules:
  0.0 493.8 jit_solution(12925493245137740278)
XLA Ops:
  6.5 1.4 convert_reduce_fusion.1
  7.9 1.3 fusion.35
  9.3 2.1 fusion.38
  13.8 6.2 %gather_fusion = s32[1024]{0:T(1024)S(1)} fusion(s32[257]{0:T(512)} %param.36, s32[1024]{0:T(1024)S(1)} %maximum_clamp_fusion), kind=kCustom, calls=%fused_computation | custom fusion | bytes 12288 | tf_op jit(solution)/shard_map/jit(_take)/gather | solution.py:34
  20.8 64.1 %all-gather.3.cloned.1.call-done = bf16[1024,4096]{1,0:T(8,128)(2,1)} async-done(((bf16[64,4096]{1,0:T(8,128)(2,1)}), bf16[1024,4096]{1,0:T(8,128)(2,1)}) %all-gather.3.cloned.1.call-update) | async-done | bytes 8388624 | tf_op jit(solution)/shard_map/all_gather | solution.py:102
  84.9 6.3 %fusion.67 = f32[1024,128]{0,1:T(8,128)S(1)} fusion(bf16[1024,4096]{1,0:T(8,128)(2,1)} %all-gather.3.cloned.1.call-done, bf16[4096,128]{1,0:T(8,128)(2,1)S(1)} %copy-done.2), kind=kOutput, calls=%fused_computation.113 | convolution fusion | flops 1073741824 | bytes 9961472 | tf_op jit(solution)/shard_map/dot_general | solution.py:16
  92.5 80.1 %all-reduce.4.cloned.1.call-done = bf16[1024,32]{0,1:T(8,128)(2,1)} async-done(((bf16[1024,32]{0,1:T(8,128)(2,1)}), bf16[1024,32]{0,1:T(8,128)(2,1)}) %all-reduce.4.cloned.1.call-update) | async-done | bytes 65552 | tf_op jit(solution)/shard_map/psum | solution.py:117
  173.4 1.8 broadcast_select_fusion
  175.2 3.3 fusion.29
  178.5 11.0 %fusion.66 = (bf16[1024,1,768]{0,2,1:T(8,128)(2,1)S(1)}, f32[1024,1,768]{0,2,1:T(8,128)S(1)}) fusion(f32[1024,768]{0,1:T(8,128)S(1)} %fusion.29, bf16[1024,4096]{1,0:T(8,128)(2,1)} %all-gather.3.cloned.1.call-done, bf16[4096,1,768]{2,0,1:T(8,128)(2,1)} %param.23), kind=kOutput, calls=%fused_computation.112 | convolution fusion | flops 6444023808 | bytes 22544384 | tf_op jit(solution)/shard_map/dot_general | solution.py:16
  190.4 2.0 reshape.569
  192.4 1.6 fusion.63
  194.0 2.0 reshape.568
  197.0 2.2 fusion.57
  206.1 2.0 copy.47
  208.2 11.3 %fusion.68 = f32[1024,512]{1,0:T(8,128)} fusion(bf16[1024,4096]{1,0:T(8,128)(2,1)} %all-gather.3.cloned.1.call-done, bf16[4096,512]{1,0:T(8,128)(2,1)} %param.25), kind=kOutput, calls=%fused_computation.114 | convolution fusion | flops 4294967296 | bytes 14680064 | tf_op jit(solution)/shard_map/dot_general | solution.py:16
  220.6 4.5 fusion.24
  225.1 1.3 fusion.70
  226.5 2.4 fusion.16
  228.9 8.3 %fusion.69 = f32[1024,4096]{1,0:T(8,128)} fusion(bf16[1024,512]{1,0:T(8,128)(2,1)S(1)} %fusion.24, bf16[512,4096]{1,0:T(8,128)(2,1)S(1)} %copy-done.9), kind=kOutput, calls=%fused_computation.115 | convolution fusion | flops 4294967296 | bytes 22020096 | tf_op jit(solution)/shard_map/dot_general | solution.py:16
  237.2 14.0 %all-gather.5.cloned.1.call-done = bf16[2,8192,256]{1,2,0:T(8,128)(2,1)} async-done(((bf16[2,1024,256]{1,2,0:T(8,128)(2,1)}), bf16[2,8192,256]{1,2,0:T(8,128)(2,1)}) %all-gather.5.cloned.1.call-update) | async-done | bytes 8388624 | tf_op jit(solution)/shard_map/all_gather | solution.py:151
  251.2 49.0 %conditional.1 = (f32[1024,1]{0,1:T(1,128)S(1)}, f32[1024,1,256]{2,0,1:T(8,128)S(1)}) conditional(s32[]{:T(128)} %convert_element_type.83, () %tuple.13, (s32[8192]{0:T(1024)S(1)}, s32[1024]{0:T(1024)S(1)}, s32[8192]{0:T(1024)S(1)}, s32[]{:T(128)}, s32[1024]{0:T(1024)S(1)}, /*index=5*/bf16[2,8192,256]{1,2,0:T(8,128)(2,1)}, ...), branch_computations={%region_9.10_spmd, %region_10.13_spmd} | conditional | flops 8774483968 | bytes 129753136 | solution.py:182
  251.2 12.0 %copy.45 = bf16[2,8192,256]{2,1,0:T(8,128)(2,1)} copy(bf16[2,8192,256]{1,2,0:T(8,128)(2,1)} %get-tuple-element.65) | data formatting | bytes 16777216 | tf_op jit(solution)/shard_map
  263.2 10.0 %fusion = (f32[1024]{0:T(1024)S(1)}, f32[8192,1024]{1,0:T(8,128)S(1)}) fusion(s32[1024]{0:T(1024)S(1)} %broadcast_add_fusion, s32[1024]{0:T(1024)S(1)} %get-tuple-element.22, s32[8192]{0:T(1024)S(1)} %get-tuple-element.23, s32[8192]{0:T(1024)S(1)} %get-tuple-element.21, bf16[1024,1,256]{0,2,1:T(8,128)(2,1)S(1)} %copy-done.4, bf16[2,8192,256]{2,1,0:T(8,128)(2,1)} %copy.45), kind=kOutput, calls=%fused_computation.4 | convolution fusion | flops 4345297920 | bytes 38350848 | tf_op jit(solution)/shard_map/cond/branch_1_fun/qhd,khd->qhk/dot_general | solution.py:164
  273.2 14.2 %fusion.7 = f32[1024,1,256]{2,0,1:T(8,128)S(1)} fusion(bf16[2,8192,256]{2,1,0:T(8,128)(2,1)} %copy.45, f32[8192,1024]{1,0:T(8,128)S(1)} %get-tuple-element.70, f32[1024]{0:T(1024)S(1)} %broadcast_maximum_fusion, s32[1024]{0:T(1024)S(1)} %broadcast_add_fusion, s32[1024]{0:T(1024)S(1)} %get-tuple-element.22, s32[8192]{0:T(1024)S(1)} %get-tuple-element.23, ...), kind=kOutput, calls=%fused_computation.12 | convolution fusion | flops 4362076160 | bytes 38875136 | tf_op jit(solution)/shard_map/cond/branch_1_fun/qhk,khd->qhd/dot_general | solution.py:174
  287.4 12.8 %fusion.2 = f32[1024]{0:T(1024)S(1)} fusion(f32[8192,1024]{1,0:T(8,128)S(1)} %get-tuple-element.70, f32[1024]{0:T(1024)S(1)} %broadcast_maximum_fusion, s32[1024]{0:T(1024)S(1)} %broadcast_add_fusion, s32[1024]{0:T(1024)S(1)} %get-tuple-element.22, s32[8192]{0:T(1024)S(1)} %get-tuple-element.23, s32[8192]{0:T(1024)S(1)} %get-tuple-element.21), kind=kLoop, calls=%fused_computation.6 | loop fusion | flops 67107840 | bytes 33636352 | tf_op jit(solution)/shard_map/cond/branch_1_fun/reduce_sum | solution.py:173
  300.2 1.9 multiply_reduce_fusion
  302.9 8.1 %fusion.25 = f32[1024,4096]{1,0:T(8,128)} fusion(bf16[1,256,4096]{2,1,0:T(8,128)(2,1)S(1)} %copy-done, f32[1024,1,256]{2,0,1:T(8,128)S(1)} %get-tuple-element.30, f32[1024]{0:T(1024)S(1)} %bitcast.116), kind=kOutput, calls=%fused_computation.37 | convolution fusion | flops 2148007936 | bytes 19927040 | tf_op jit(solution)/shard_map/dot_general | solution.py:16
  311.0 73.2 %all-reduce.6.cloned.1.call-done = bf16[1024,32]{0,1:T(8,128)(2,1)} async-done(((bf16[1024,32]{0,1:T(8,128)(2,1)}), bf16[1024,32]{0,1:T(8,128)(2,1)}) %all-reduce.6.cloned.1.call-update) | async-done | bytes 65552 | tf_op jit(solution)/shard_map/psum | solution.py:201
  385.0 15.6 %add_convert_fusion = bf16[1024,4096]{1,0:T(8,128)(2,1)} fusion(f32[1024,4096]{1,0:T(8,128)} %fusion.25, f32[1024,4096]{1,0:T(8,128)} %fusion.69, bf16[1024,128]{0,1:T(8,128)(2,1)S(1)} %bitcast.112, bf16[128,4096]{1,0:T(8,128)(2,1)} %param.34), kind=kOutput, calls=%fused_computation.19 | convolution fusion | flops 1086324736 | bytes 43253760 | tf_op jit(solution)/shard_map/dot_general | solution.py:16
  400.7 84.6 %reduce-scatter.2.cloned.1.call-done = bf16[64,4096]{1,0:T(8,128)(2,1)} async-done(((bf16[1024,4096]{1,0:T(8,128)(2,1)}), bf16[64,4096]{1,0:T(8,128)(2,1)}) %reduce-scatter.2.cloned.1.call-update) | async-done | bytes 524304 | tf_op jit(solution)/shard_map/reduce_scatter | solution.py:203
  485.3 2.0 fusion.40
  (75 shorter events, 15.5 us)
Async XLA Ops:
  6.5 296.3 %copy-start = (bf16[1,256,4096]{2,1,0:T(8,128)(2,1)S(1)}, bf16[1,256,4096]{2,1,0:T(8,128)(2,1)}, u32[]{:S(2)}) copy-start(bf16[1,256,4096]{2,1,0:T(8,128)(2,1)} %param.24) | copy-start | bytes 6291460
  6.5 13.5 %copy-start.8 = (s32[4]{0:T(128)S(1)}, s32[4]{0:T(128)}, u32[]{:S(2)}) copy-start(s32[4]{0:T(128)} %param.37) | copy-start | bytes 52
  6.5 78.4 %copy-start.2 = (bf16[4096,128]{1,0:T(8,128)(2,1)S(1)}, bf16[4096,128]{1,0:T(8,128)(2,1)}, u32[]{:S(2)}) copy-start(bf16[4096,128]{1,0:T(8,128)(2,1)} %param.29) | copy-start | bytes 3145732
  6.5 78.4 %all-gather.3.cloned.1.call-start = ((), (), s32[]{:S(2)}) async-start(), calls=%async_computation.1 | async-start | bytes 8912896 | tf_op jit(solution)/shard_map/all_gather | solution.py:102
  11.4 161.2 %all-reduce.4.cloned.1.call-start = ((), (), s32[]{:S(2)}) async-start(), calls=%async_computation.2 | async-start | bytes 131072 | tf_op jit(solution)/shard_map/psum | solution.py:117
  91.9 159.3 %all-gather.5.cloned.1.call-start = ((), (), s32[]{:S(2)}) async-start(), calls=%async_computation.3 | async-start | bytes 9437184 | tf_op jit(solution)/shard_map/all_gather | solution.py:151
  202.1 182.1 %all-reduce.6.cloned.1.call-start = ((), (), s32[]{:S(2)}) async-start(), calls=%async_computation.4 | async-start | bytes 131072 | tf_op jit(solution)/shard_map/psum | solution.py:201
  208.2 11.3 %copy-start.5 = (bf16[1024,1,32,1]{0,2,3,1:T(8,128)(2,1)S(1)}, bf16[1024,1,32,1]{0,2,3,1:T(8,128)(2,1)}, u32[]{:S(2)}) copy-start(bf16[1024,1,32,1]{0,2,3,1:T(8,128)(2,1)} %get-tuple-element.75) | copy-start | bytes 196612
  208.2 11.3 %copy-start.6 = (bf16[1024,1,32,1]{0,2,3,1:T(8,128)(2,1)S(1)}, bf16[1024,1,32,1]{0,2,3,1:T(8,128)(2,1)}, u32[]{:S(2)}) copy-start(bf16[1024,1,32,1]{0,2,3,1:T(8,128)(2,1)} %get-tuple-element.76) | copy-start | bytes 196612
  208.2 12.4 %copy-start.11 = (f32[512]{0:T(512)S(1)}, f32[512]{0:T(512)}, u32[]{:S(2)}) copy-start(f32[512]{0:T(512)} %param.26) | copy-start | bytes 6148
  220.6 4.6 copy-start.10
  225.1 1.4 copy-start.3
  225.1 3.8 copy-start.9
  251.2 12.0 %copy-start.4 = (bf16[1024,1,256]{0,2,1:T(8,128)(2,1)S(1)}, bf16[1024,1,256]{0,2,1:T(8,128)(2,1)}, u32[]{:S(2)}) copy-start(bf16[1024,1,256]{0,2,1:T(8,128)(2,1)} %get-tuple-element.66) | copy-start | bytes 1572868 | tf_op jit(solution)/shard_map/cond
  302.8 182.5 %reduce-scatter.2.cloned.1.call-start = ((), (), s32[]{:S(2)}) async-start(), calls=%async_computation.5 | async-start | bytes 8912896 | tf_op jit(solution)/shard_map/reduce_scatter | solution.py:203
  400.6 84.7 %copy-start.1 = (bf16[64,4096]{1,0:T(8,128)(2,1)S(1)}, bf16[64,4096]{1,0:T(8,128)(2,1)}, u32[]{:S(2)}) copy-start(bf16[64,4096]{1,0:T(8,128)(2,1)} %param.20) | copy-start | bytes 1572868
  400.6 84.7 %copy-start.7 = (f32[4096]{0:T(1024)S(1)}, f32[4096]{0:T(1024)}, u32[]{:S(2)}) copy-start(f32[4096]{0:T(1024)} %param.28) | copy-start | bytes 49156
Sparse Core Ops, SparseCore 0:
  11.5 73.3 all-gather.2
  92.0 80.5 all-reduce.3
  202.2 48.9 all-gather.4
  302.9 81.1 all-reduce.5
  400.8 84.4 reduce-scatter.1
where the time goes:
time: 495 us; the launch traced here: 494 us
  waiting for transfers between devices  316 us (64%)
  matrix products  95.9 us (19%)
  other arithmetic  34.2 us (7%)
  local copies, waits for them, and re-layouts  32.5 us (7%)
  between operations  14.7 us (3%)
    reduce_scatter x1, waiting for transfers between devices, per_device(): lax.psum_scatter((rank_product(attention_output, output_rows) + (rank_pro...  84.6 us
    psum x1, waiting for transfers between devices, per_device(): rank_input = lax.psum(rank_part.astype(jnp.bfloat16), 'mlp')  80.1 us
    psum x1, waiting for transfers between devices, per_device(): rank_output = lax.psum(rank_part_out.astype(jnp.bfloat16), 'mlp')  73.2 us
    dot_general x10, matrix products, rank_product(): return jnp.dot(left_side, right_side, preferred_element_type=jnp.float32)  71.7 us
    all_gather x1, waiting for transfers between devices, per_device(): slot_portion = lax.all_gather(normed_rows, 'mlp', axis=0, tiled=True)  64.1 us
    dot_general x1, matrix products, attend(): jnp.einsum('qhk,khd->qhd', weights.astype(jnp.bfloat16), part_values, pre...  14.2 us
    all_gather x1, waiting for transfers between devices, per_device(): slot_portion = lax.all_gather(paired, 'req', axis=1, tiled=True)  14 us
    reduce_sum x1, other arithmetic, attend(): new_total = jnp.sum(weights, axis=2)  12.8 us
  transfers between devices with their start and end apart: 5, of which 5 were waited for; matrix products, arithmetic and copies ran while one was open for 10% of the time, Pallas kernels for 0%

commit v1 on v0

--- a/solution.py
+++ b/solution.py
@@ -114,7 +114,7 @@
     rank_part = slot_selector(
         grouped[:, query_key_columns + hid_local :], slot_adapter, adapter_id, 2 * ADAPTER_RANK
     )
-    rank_input = lax.psum(rank_part.astype(jnp.bfloat16), "mlp")
+    rank_input = jnp.sum(lax.all_gather(rank_part.astype(jnp.bfloat16), "mlp"), axis=0)
     qkv_extra = rank_product(
         widen_rows(rank_input[:, :ADAPTER_RANK], every_id, adapter_id),
         query_key_value_right.reshape(adapter_ids * ADAPTER_RANK, query_key_columns),

time: 495 us -> 462 us (0.933)
  waiting for transfers between devices: 316 us -> 278 us
    psum x1 -> x0, waiting for transfers between devices: 80.1 us -> none  [per_device(): rank_input = lax.psum(rank_part.astype(jnp.bfloat16), 'mlp')]
    all_gather x0 -> x1, waiting for transfers between devices: none -> 41.1 us  [per_device(): lax.all_gather(rank_part.astype(jnp.bfloat16), 'mlp')]
  transfers between devices with their start and end apart: 5 -> 5, of which waited for: 5 -> 5; matrix products, arithmetic and copies ran while one was open for 10% -> 11% of each run, Pallas kernels for 0% -> 0%
where the time goes in v1:
time: 462 us; the launch traced here: 461 us
  waiting for transfers between devices  278 us (60%)
  matrix products  96.2 us (21%)
  local copies, waits for them, and re-layouts  36.7 us (8%)
  other arithmetic  34.8 us (8%)
  between operations  14.6 us (3%)
    reduce_scatter x1, waiting for transfers between devices, per_device(): lax.psum_scatter((rank_product(attention_output, output_rows) + (rank_pro...  84.6 us
    psum x1, waiting for transfers between devices, per_device(): rank_output = lax.psum(rank_part_out.astype(jnp.bfloat16), 'mlp')  73.2 us
    dot_general x10, matrix products, rank_product(): return jnp.dot(left_side, right_side, preferred_element_type=jnp.float32)  72 us
    all_gather x1, waiting for transfers between devices, per_device(): slot_portion = lax.all_gather(normed_rows, 'mlp', axis=0, tiled=True)  64.8 us
    all_gather x1, waiting for transfers between devices, per_device(): lax.all_gather(rank_part.astype(jnp.bfloat16), 'mlp')  41.1 us
    dot_general x1, matrix products, attend(): jnp.einsum('qhk,khd->qhd', weights.astype(jnp.bfloat16), part_values, pre...  14.2 us
    all_gather x1, waiting for transfers between devices, per_device(): slot_portion = lax.all_gather(paired, 'req', axis=1, tiled=True)  14.1 us
    reduce_sum x1, other arithmetic, attend(): new_total = jnp.sum(weights, axis=2)  12.8 us
  transfers between devices with their start and end apart: 5, of which 5 were waited for; matrix products, arithmetic and copies ran while one was open for 11% of the time, Pallas kernels for 0%

profile of v1, /device:TPU:0, one launch (start us, length us, event | category | flops | bytes accessed | tf_op | source)
XLA Modules:
  0.0 460.7 jit_solution(13348844906701253270)
XLA Ops:
  6.5 1.4 convert_reduce_fusion.1
  9.3 2.1 fusion.38
  13.8 6.2 %gather_fusion = s32[1024]{0:T(1024)S(1)} fusion(s32[257]{0:T(512)} %param.36, s32[1024]{0:T(1024)S(1)} %maximum_clamp_fusion), kind=kCustom, calls=%fused_computation | custom fusion | bytes 12288 | tf_op jit(solution)/shard_map/jit(_take)/gather | solution.py:34
  20.1 64.8 %all-gather.5.cloned.1.call-done = bf16[1024,4096]{1,0:T(8,128)(2,1)} async-done(((bf16[64,4096]{1,0:T(8,128)(2,1)}), bf16[1024,4096]{1,0:T(8,128)(2,1)}) %all-gather.5.cloned.1.call-update) | async-done | bytes 8388624 | tf_op jit(solution)/shard_map/all_gather | solution.py:102
  84.9 6.3 %fusion.67 = f32[1024,128]{0,1:T(8,128)S(1)} fusion(bf16[1024,4096]{1,0:T(8,128)(2,1)} %all-gather.5.cloned.1.call-done, bf16[4096,128]{1,0:T(8,128)(2,1)S(1)} %copy-done.2), kind=kOutput, calls=%fused_computation.114 | convolution fusion | flops 1073741824 | bytes 9961472 | tf_op jit(solution)/shard_map/dot_general | solution.py:16
  93.4 41.1 %all-gather.9.cloned.1.call-done = bf16[16384,32]{0,1:T(8,128)(2,1)} async-done(((bf16[1024,32]{0,1:T(8,128)(2,1)}), bf16[16384,32]{0,1:T(8,128)(2,1)}) %all-gather.9.cloned.1.call-update) | async-done | bytes 1048592 | tf_op jit(solution)/shard_map/all_gather | solution.py:117
  134.5 1.9 copy.59
  137.0 1.8 broadcast_select_fusion
  138.8 3.6 fusion.29
  142.4 11.0 %fusion.66 = (bf16[1024,1,768]{0,2,1:T(8,128)(2,1)}, f32[1024,1,768]{0,2,1:T(8,128)}) fusion(f32[1024,768]{0,1:T(8,128)} %fusion.29, bf16[1024,4096]{1,0:T(8,128)(2,1)S(1)} %bitcast.114, bf16[4096,1,768]{2,0,1:T(8,128)(2,1)} %param.23), kind=kOutput, calls=%fused_computation.113 | convolution fusion | flops 6444023808 | bytes 22544384 | tf_op jit(solution)/shard_map/dot_general | solution.py:16
  155.6 1.9 fusion.61
  157.5 1.9 reshape.577
  159.4 1.6 fusion.63
  161.1 2.0 reshape.576
  164.0 2.2 fusion.57
  173.0 2.0 copy.52
  175.1 11.3 %fusion.68 = f32[1024,512]{1,0:T(8,128)} fusion(bf16[1024,4096]{1,0:T(8,128)(2,1)} %all-gather.5.cloned.1.call-done, bf16[4096,512]{1,0:T(8,128)(2,1)} %param.25), kind=kOutput, calls=%fused_computation.115 | convolution fusion | flops 4294967296 | bytes 14680064 | tf_op jit(solution)/shard_map/dot_general | solution.py:16
  187.5 4.5 fusion.24
  193.4 2.4 fusion.16
  195.8 8.3 %fusion.69 = f32[1024,4096]{1,0:T(8,128)} fusion(bf16[1024,512]{1,0:T(8,128)(2,1)S(1)} %fusion.24, bf16[512,4096]{1,0:T(8,128)(2,1)S(1)} %copy-done.9), kind=kOutput, calls=%fused_computation.116 | convolution fusion | flops 4294967296 | bytes 22020096 | tf_op jit(solution)/shard_map/dot_general | solution.py:16
  204.1 14.1 %all-gather.7.cloned.1.call-done = bf16[2,8192,256]{1,2,0:T(8,128)(2,1)} async-done(((bf16[2,1024,256]{1,2,0:T(8,128)(2,1)}), bf16[2,8192,256]{1,2,0:T(8,128)(2,1)}) %all-gather.7.cloned.1.call-update) | async-done | bytes 8388624 | tf_op jit(solution)/shard_map/all_gather | solution.py:151
  218.2 49.0 %conditional.1 = (f32[1024,1]{0,1:T(1,128)S(1)}, f32[1024,1,256]{2,0,1:T(8,128)S(1)}) conditional(s32[]{:T(128)} %convert_element_type.95, () %tuple.13, (s32[8192]{0:T(1024)S(1)}, s32[1024]{0:T(1024)S(1)}, s32[8192]{0:T(1024)S(1)}, s32[]{:T(128)}, s32[1024]{0:T(1024)S(1)}, /*index=5*/bf16[2,8192,256]{1,2,0:T(8,128)(2,1)}, ...), branch_computations={%region_9.10_spmd, %region_10.13_spmd} | conditional | flops 8774483968 | bytes 129753136 | solution.py:182
  218.2 12.0 %copy.50 = bf16[2,8192,256]{2,1,0:T(8,128)(2,1)} copy(bf16[2,8192,256]{1,2,0:T(8,128)(2,1)} %get-tuple-element.72) | data formatting | bytes 16777216 | tf_op jit(solution)/shard_map
  230.2 10.0 %fusion = (f32[1024]{0:T(1024)S(1)}, f32[8192,1024]{1,0:T(8,128)S(1)}) fusion(s32[1024]{0:T(1024)S(1)} %broadcast_add_fusion, s32[1024]{0:T(1024)S(1)} %get-tuple-element.22, s32[8192]{0:T(1024)S(1)} %get-tuple-element.23, s32[8192]{0:T(1024)S(1)} %get-tuple-element.21, bf16[1024,1,256]{0,2,1:T(8,128)(2,1)S(1)} %copy-done.4, bf16[2,8192,256]{2,1,0:T(8,128)(2,1)} %copy.50), kind=kOutput, calls=%fused_computation.4 | convolution fusion | flops 4345297920 | bytes 38350848 | tf_op jit(solution)/shard_map/cond/branch_1_fun/qhd,khd->qhk/dot_general | solution.py:164
  240.2 14.2 %fusion.7 = f32[1024,1,256]{2,0,1:T(8,128)S(1)} fusion(bf16[2,8192,256]{2,1,0:T(8,128)(2,1)} %copy.50, f32[8192,1024]{1,0:T(8,128)S(1)} %get-tuple-element.77, f32[1024]{0:T(1024)S(1)} %broadcast_maximum_fusion, s32[1024]{0:T(1024)S(1)} %broadcast_add_fusion, s32[1024]{0:T(1024)S(1)} %get-tuple-element.22, s32[8192]{0:T(1024)S(1)} %get-tuple-element.23, ...), kind=kOutput, calls=%fused_computation.12 | convolution fusion | flops 4362076160 | bytes 38875136 | tf_op jit(solution)/shard_map/cond/branch_1_fun/qhk,khd->qhd/dot_general | solution.py:174
  254.4 12.8 %fusion.2 = f32[1024]{0:T(1024)S(1)} fusion(f32[8192,1024]{1,0:T(8,128)S(1)} %get-tuple-element.77, f32[1024]{0:T(1024)S(1)} %broadcast_maximum_fusion, s32[1024]{0:T(1024)S(1)} %broadcast_add_fusion, s32[1024]{0:T(1024)S(1)} %get-tuple-element.22, s32[8192]{0:T(1024)S(1)} %get-tuple-element.23, s32[8192]{0:T(1024)S(1)} %get-tuple-element.21), kind=kLoop, calls=%fused_computation.6 | loop fusion | flops 67107840 | bytes 33636352 | tf_op jit(solution)/shard_map/cond/branch_1_fun/reduce_sum | solution.py:173
  267.2 1.9 multiply_reduce_fusion
  269.9 8.1 %fusion.25 = f32[1024,4096]{1,0:T(8,128)} fusion(bf16[1,256,4096]{2,1,0:T(8,128)(2,1)S(1)} %copy-done, f32[1024,1,256]{2,0,1:T(8,128)S(1)} %get-tuple-element.30, f32[1024]{0:T(1024)S(1)} %bitcast.124), kind=kOutput, calls=%fused_computation.37 | convolution fusion | flops 2148007936 | bytes 19927040 | tf_op jit(solution)/shard_map/dot_general | solution.py:16
  278.0 73.2 %all-reduce.3.cloned.1.call-done = bf16[1024,32]{0,1:T(8,128)(2,1)} async-done(((bf16[1024,32]{0,1:T(8,128)(2,1)}), bf16[1024,32]{0,1:T(8,128)(2,1)}) %all-reduce.3.cloned.1.call-update) | async-done | bytes 65552 | tf_op jit(solution)/shard_map/psum | solution.py:201
  352.0 15.6 %add_convert_fusion = bf16[1024,4096]{1,0:T(8,128)(2,1)} fusion(f32[1024,4096]{1,0:T(8,128)} %fusion.25, f32[1024,4096]{1,0:T(8,128)} %fusion.69, bf16[1024,128]{0,1:T(8,128)(2,1)S(1)} %bitcast.119, bf16[128,4096]{1,0:T(8,128)(2,1)} %param.34), kind=kOutput, calls=%fused_computation.19 | convolution fusion | flops 1086324736 | bytes 43253760 | tf_op jit(solution)/shard_map/dot_general | solution.py:16
  367.7 84.6 %reduce-scatter.2.cloned.1.call-done = bf16[64,4096]{1,0:T(8,128)(2,1)} async-done(((bf16[1024,4096]{1,0:T(8,128)(2,1)}), bf16[64,4096]{1,0:T(8,128)(2,1)}) %reduce-scatter.2.cloned.1.call-update) | async-done | bytes 524304 | tf_op jit(solution)/shard_map/reduce_scatter | solution.py:203
  452.2 2.0 fusion.40
  (84 shorter events, 19.3 us)
Async XLA Ops:
  6.5 263.3 %copy-start = (bf16[1,256,4096]{2,1,0:T(8,128)(2,1)S(1)}, bf16[1,256,4096]{2,1,0:T(8,128)(2,1)}, u32[]{:S(2)}) copy-start(bf16[1,256,4096]{2,1,0:T(8,128)(2,1)} %param.24) | copy-start | bytes 6291460
  6.5 13.5 %copy-start.8 = (s32[4]{0:T(128)S(1)}, s32[4]{0:T(128)}, u32[]{:S(2)}) copy-start(s32[4]{0:T(128)} %param.37) | copy-start | bytes 52
  6.5 78.4 %copy-start.2 = (bf16[4096,128]{1,0:T(8,128)(2,1)S(1)}, bf16[4096,128]{1,0:T(8,128)(2,1)}, u32[]{:S(2)}) copy-start(bf16[4096,128]{1,0:T(8,128)(2,1)} %param.29) | copy-start | bytes 3145732
  6.5 78.4 %all-gather.5.cloned.1.call-start = ((), (), s32[]{:S(2)}) async-start(), calls=%async_computation.1 | async-start | bytes 8912896 | tf_op jit(solution)/shard_map/all_gather | solution.py:102
  11.4 123.1 %all-gather.9.cloned.1.call-start = ((), (), s32[]{:S(2)}) async-start(), calls=%async_computation.5 | async-start | bytes 1114112 | tf_op jit(solution)/shard_map/all_gather | solution.py:117
  91.9 126.3 %all-gather.7.cloned.1.call-start = ((), (), s32[]{:S(2)}) async-start(), calls=%async_computation.2 | async-start | bytes 9437184 | tf_op jit(solution)/shard_map/all_gather | solution.py:151
  134.5 4.3 copy-start.10
  136.4 6.0 %slice-start = ((s8[8388608]{0:T(1024)(128)(4,1)}), s8[4194304]{0:T(1024)(128)(4,1)S(1)}, s32[]{:S(2)}) async-start(s8[8388608]{0:T(1024)(128)(4,1)} %bitcast.113), calls=%async_computation.6 | async-start | bytes 8388608
  138.8 3.6 slice-start.1
  169.1 182.0 %all-reduce.3.cloned.1.call-start = ((), (), s32[]{:S(2)}) async-start(), calls=%async_computation.3 | async-start | bytes 131072 | tf_op jit(solution)/shard_map/psum | solution.py:201
  175.1 11.3 %copy-start.5 = (bf16[1024,1,32,1]{0,2,3,1:T(8,128)(2,1)S(1)}, bf16[1024,1,32,1]{0,2,3,1:T(8,128)(2,1)}, u32[]{:S(2)}) copy-start(bf16[1024,1,32,1]{0,2,3,1:T(8,128)(2,1)} %get-tuple-element.82) | copy-start | bytes 196612
  175.1 11.3 %copy-start.6 = (bf16[1024,1,32,1]{0,2,3,1:T(8,128)(2,1)S(1)}, bf16[1024,1,32,1]{0,2,3,1:T(8,128)(2,1)}, u32[]{:S(2)}) copy-start(bf16[1024,1,32,1]{0,2,3,1:T(8,128)(2,1)} %get-tuple-element.83) | copy-start | bytes 196612
  175.1 12.4 %copy-start.12 = (f32[512]{0:T(512)S(1)}, f32[512]{0:T(512)}, u32[]{:S(2)}) copy-start(f32[512]{0:T(512)} %param.26) | copy-start | bytes 6148
  187.5 4.5 copy-start.11
  192.0 1.4 copy-start.3
  192.1 3.8 copy-start.9
  218.2 12.0 %copy-start.4 = (bf16[1024,1,256]{0,2,1:T(8,128)(2,1)S(1)}, bf16[1024,1,256]{0,2,1:T(8,128)(2,1)}, u32[]{:S(2)}) copy-start(bf16[1024,1,256]{0,2,1:T(8,128)(2,1)} %get-tuple-element.73) | copy-start | bytes 1572868 | tf_op jit(solution)/shard_map/cond
  269.8 182.4 %reduce-scatter.2.cloned.1.call-start = ((), (), s32[]{:S(2)}) async-start(), calls=%async_computation.4 | async-start | bytes 8912896 | tf_op jit(solution)/shard_map/reduce_scatter | solution.py:203
  367.6 84.6 %copy-start.1 = (bf16[64,4096]{1,0:T(8,128)(2,1)S(1)}, bf16[64,4096]{1,0:T(8,128)(2,1)}, u32[]{:S(2)}) copy-start(bf16[64,4096]{1,0:T(8,128)(2,1)} %param.20) | copy-start | bytes 1572868
  367.6 84.6 %copy-start.7 = (f32[4096]{0:T(1024)S(1)}, f32[4096]{0:T(1024)}, u32[]{:S(2)}) copy-start(f32[4096]{0:T(1024)} %param.28) | copy-start | bytes 49156
Sparse Core Ops, SparseCore 0:
  11.5 73.3 all-gather.4
  92.0 42.4 all-gather.8
  169.2 48.8 all-gather.6
  269.9 81.1 all-reduce.2
  367.8 84.3 reduce-scatter.1
